TPU v7x, 256 devices: a whole 4x4x8 slice. The times are simulated.
256 devices in a mesh: ga: 4 (over z_hi), orb: 64 (over x, z_lo, y, core).
Axes of the slice: x: 4, y: 4, z: 8 (z_hi: 4, z_lo: 2; z = z_hi * 2 + z_lo), core: 2. Of those that a mesh axis runs over, the one named last changes fastest.
Arguments:
- coefficients: bfloat16 [2, 294912, 512], P(None, ('ga', 'orb')), may hold values from -0.01171875 to 0.01171875
- triples: int32 [3, 294912], P(None, ('ga', 'orb')), may hold values from -33 to 33
- elec_pos: float32 [3, 256], P(None, ('ga', 'orb')), may hold values from 0 to 1
- ion_pos: float32 [3, 128], replicated, may hold values from 0 to 1
- assignment: int32 [256], P(('ga', 'orb')), may hold values from 0 to 127
- rotation: int32 [256], P(('ga', 'orb')), may hold values from 0 to 63
- quad_table: float32 [64, 3, 12], replicated, may hold values from -2.4 to 2.4
- inverse_rows: float32 [256, 512], P(('ga', 'orb')), may hold values from -0.25 to 0.25
Outputs:
- ratios: float32 [256, 12], P(('ga', 'orb'))
All inputs are finite; a program needn't handle non-finite values.
Results may differ from a plain program's by a relative error of at most 0.0024.
Values may be sent and summed in bfloat16 or wider, within the bound.
No kernel may reach another device: no remote copies, remote signals or barrier semaphores. Data moves between devices by JAX's collectives and lax.ppermute only.
A program may use at most 64 MiB of HBM per device.

v0:
```python
import math
import jax
import jax.numpy as jnp
from jax import lax
from jax.sharding import PartitionSpec as P

TWO_PI = 2.0 * math.pi


def point_coords(elec_pos, ion_pos, assignment, rotation, quad_table):
    ion_rows = jnp.take(ion_pos, assignment, axis=1)
    offsets = elec_pos - ion_rows
    radius = jnp.sqrt(jnp.sum(offsets * offsets, axis=0))
    displace = jnp.take(quad_table, rotation, axis=0)
    located = ion_rows.T[:, :, None] + radius[:, None, None] * displace
    return jnp.transpose(located, (1, 0, 2)).reshape(3, -1)


def phase_values(points, triples, coefficients):
    point_count = points.shape[1]
    wave_count = triples.shape[1]
    columns = coefficients.shape[2]
    block_rows = math.gcd(point_count, 512)
    waves = triples.astype(jnp.float32) * TWO_PI

    def one_block(block_points):

        def add_panel(step_index, running):
            angle = (
                block_points[0][:, None] * waves[0][None, :]
                + block_points[1][:, None] * waves[1][None, :]
                + block_points[2][:, None] * waves[2][None, :]
            )
            phases = jnp.concatenate(
                [jnp.cos(angle).astype(jnp.bfloat16), jnp.sin(angle).astype(jnp.bfloat16)], axis=1
            )
            weights = coefficients.reshape(2 * wave_count, columns)
            return running + jnp.dot(phases, weights, preferred_element_type=jnp.float32)

        initial = jnp.zeros((block_rows, columns), jnp.float32)
        return lax.fori_loop(0, wave_count // wave_count, add_panel, initial)

    blocks = jnp.transpose(points.reshape(3, point_count // block_rows, block_rows), (1, 0, 2))
    return lax.map(one_block, blocks).reshape(point_count, columns)


def on_device(
    coefficients, triples, elec_pos, ion_pos, assignment, rotation, quad_table, inverse_rows
):
    local_points = point_coords(elec_pos, ion_pos, assignment, rotation, quad_table)
    all_points = lax.all_gather(local_points, ("ga", "orb"), axis=1, tiled=True)
    electrons = inverse_rows.shape[0]
    values = lax.psum_scatter(
        phase_values(all_points, triples, coefficients),
        ("ga", "orb"),
        scatter_dimension=0,
        tiled=True,
    )
    shaped = values.reshape(electrons, values.shape[0] // electrons, values.shape[1])
    return jnp.sum(shaped * inverse_rows[:, None, :], axis=2)


def solution(mesh):
    return jax.shard_map(
        on_device,
        mesh=mesh,
        in_specs=(
            P(None, ("ga", "orb"), None),
            P(None, ("ga", "orb")),
            P(None, ("ga", "orb")),
            P(),
            P(("ga", "orb")),
            P(("ga", "orb")),
            P(),
            P(("ga", "orb"), None),
        ),
        out_specs=P(("ga", "orb"), None),
        check_vma=False,
    )
```

profile of v0, /device:TPU:192, one launch (start us, length us, event | category | flops | bytes accessed | tf_op | source)
XLA Modules:
  0.0 1629.5 jit_solution(16454387211662428138)
XLA Ops:
  5.1 307.0 %all-gather = f32[256,12,3]{1,2,0:T(4,128)S(1)} all-gather(f32[1,12,3]{1,2,0:T(4,128)S(1)} %add_bitcast_fusion), channel_id=1, replica_groups=mesh['ga'=4,'orb'=64] {'ga','orb'}, dimensions={0}, use_global_device_ids=true | all-gather | bytes 37008 | tf_op jit(solution)/shard_map/all_gather | solution.py:51
  313.2 70.7 %while.16 = (s32[]{:T(128)}, f32[6,512,512]{2,1,0:T(8,128)}, f32[6,3,512]{2,0,1:T(8,128)S(1)}, f32[3,1152]{1,0:T(4,128)S(1)}, bf16[2,1152,512]{2,1,0:T(8,128)(2,1)}, /*index=5*/s32[]{:T(128)}, s32[]{:T(128)}, s32[]{}, s32[]{}) while((s32[]{:T(128)}, f32[6,512,512]{2,1,0:T(8,128)}, f32[6,3,512]{2,0,1:T(8,128)S(1)}, f32[3,1152]{1,0:T(4,128)S(1)}, ...), condition=%wide.region_2.3_spmd, body=%wide.region_1.2_spmd.sunk | while | flops 1216806912 | bytes 17624220 | solution.py:44
  383.9 646.7 %fusion = f32[16,512]{1,0:T(8,128)S(1)} fusion(f32[3072,512]{1,0:T(8,128)} %bitcast.42), kind=kCustom, calls=%all-reduce-scatter | all-reduce-scatter fusion | flops 2097153 | bytes 6324224
  1030.6 85.6 %collective-permute-start = (f32[16,512]{1,0:T(8,128)S(1)}, f32[16,512]{1,0:T(8,128)S(1)}, u32[]{:S(2)}, u32[]{:S(2)}) collective-permute-start(f32[16,512]{1,0:T(8,128)S(1)} %fusion), channel_id=1, source_target_pairs={{0,1},{1,2},{2,3},{3,4},{4,5},{5,6},{6,7},{7,8},{8,9},{9,10},{10,1... | collective-permute-start | bytes 98312
  1116.2 13.1 collective-permute-start.1
  1129.3 13.1 collective-permute-start.10
  1143.8 14.8 collective-permute-start.11
  1158.6 13.1 collective-permute-start.12
  1171.8 13.1 collective-permute-start.13
  1184.9 13.1 collective-permute-start.14
  1198.0 13.1 collective-permute-start.15
  1211.2 13.1 collective-permute-start.16
  1224.3 13.1 collective-permute-start.17
  1237.5 13.1 collective-permute-start.18
  1250.6 13.1 collective-permute-start.19
  1263.7 13.1 collective-permute-start.2
  1276.9 13.1 collective-permute-start.20
  1290.0 13.1 collective-permute-start.21
  1303.2 13.1 collective-permute-start.22
  1316.3 13.1 collective-permute-start.23
  1329.4 13.1 collective-permute-start.24
  1342.6 13.1 collective-permute-start.25
  1355.7 13.1 collective-permute-start.26
  1368.9 13.1 collective-permute-start.27
  1382.0 13.1 collective-permute-start.28
  1437.1 24.4 %collective-permute-start.4 = (f32[16,512]{1,0:T(8,128)S(1)}, f32[16,512]{1,0:T(8,128)S(1)}, u32[]{:S(2)}, u32[]{:S(2)}) collective-permute-start(f32[16,512]{1,0:T(8,128)S(1)} %fusion), channel_id=1, source_target_pairs={{0,5},{1,6},{2,7},{3,8},{4,9},{5,10},{6,11},{7,12},{8,13},{9,14},{... | collective-permute-start | bytes 98312
  1485.3 20.8 %collective-permute-start.5 = (f32[16,512]{1,0:T(8,128)S(1)}, f32[16,512]{1,0:T(8,128)S(1)}, u32[]{:S(2)}, u32[]{:S(2)}) collective-permute-start(f32[16,512]{1,0:T(8,128)S(1)} %fusion), channel_id=1, source_target_pairs={{0,6},{1,7},{2,8},{3,9},{4,10},{5,11},{6,12},{7,13},{8,14},{9,15},... | collective-permute-start | bytes 98312
  1530.3 17.3 %collective-permute-start.6 = (f32[16,512]{1,0:T(8,128)S(1)}, f32[16,512]{1,0:T(8,128)S(1)}, u32[]{:S(2)}, u32[]{:S(2)}) collective-permute-start(f32[16,512]{1,0:T(8,128)S(1)} %fusion), channel_id=1, source_target_pairs={{0,7},{1,8},{2,9},{3,10},{4,11},{5,12},{6,13},{7,14},{8,15},{9,16}... | collective-permute-start | bytes 98312
  1558.0 12.6 collective-permute-start.7
  1570.7 13.1 collective-permute-start.8
  1583.9 13.3 collective-permute-start.9
  1605.6 23.3 %concatenate.6 = f32[1036,512]{1,0:T(8,128)S(1)} concatenate(f32[12,512]{1,0:T(8,128)S(1)} %collective-permute-done.63, f32[16,512]{1,0:T(8,128)} %copy-done.18, f32[16,512]{1,0:T(8,128)} %copy-done.17, f32[16,512]{1,0:T(8,128)} %copy-done.16, f32[16,512]{1,0:T(8,128)} %copy-done.14, f32[16,512]{1,0:T(8,128)} %copy-done.13, f32[16,512]{1,0:T(8,128)} %copy-done.12, ...), dimensions={0} | concatenate | bytes 4243456
  (191 shorter events, 184.5 us)
Async XLA Ops:
  1030.6 141.2 %collective-permute-start = (f32[16,512]{1,0:T(8,128)S(1)}, f32[16,512]{1,0:T(8,128)S(1)}, u32[]{:S(2)}, u32[]{:S(2)}) collective-permute-start(f32[16,512]{1,0:T(8,128)S(1)} %fusion), channel_id=1, source_target_pairs={{0,1},{1,2},{2,3},{3,4},{4,5},{5,6},{6,7},{7,8},{8,9},{9,10},{10,1... | collective-permute-start | bytes 98312
  1116.2 68.7 %collective-permute-start.1 = (f32[16,512]{1,0:T(8,128)S(1)}, f32[16,512]{1,0:T(8,128)S(1)}, u32[]{:S(2)}, u32[]{:S(2)}) collective-permute-start(f32[16,512]{1,0:T(8,128)S(1)} %fusion), channel_id=1, source_target_pairs={{0,2},{1,3},{2,4},{3,5},{4,6},{5,7},{6,8},{7,9},{8,10},{9,11},{10,... | collective-permute-start | bytes 98312
  1129.3 68.7 %collective-permute-start.10 = (f32[16,512]{1,0:T(8,128)S(1)}, f32[16,512]{1,0:T(8,128)S(1)}, u32[]{:S(2)}, u32[]{:S(2)}) collective-permute-start(f32[16,512]{1,0:T(8,128)S(1)} %fusion), channel_id=1, source_target_pairs={{0,11},{1,12},{2,13},{3,14},{4,15},{5,16},{6,17},{7,18},{8,19},{9,... | collective-permute-start | bytes 98312
  1143.8 67.4 %collective-permute-start.11 = (f32[16,512]{1,0:T(8,128)S(1)}, f32[16,512]{1,0:T(8,128)S(1)}, u32[]{:S(2)}, u32[]{:S(2)}) collective-permute-start(f32[16,512]{1,0:T(8,128)S(1)} %fusion), channel_id=1, source_target_pairs={{0,12},{1,13},{2,14},{3,15},{4,16},{5,17},{6,18},{7,19},{8,20},{9,... | collective-permute-start | bytes 98312
  1158.6 65.7 %collective-permute-start.12 = (f32[16,512]{1,0:T(8,128)S(1)}, f32[16,512]{1,0:T(8,128)S(1)}, u32[]{:S(2)}, u32[]{:S(2)}) collective-permute-start(f32[16,512]{1,0:T(8,128)S(1)} %fusion), channel_id=1, source_target_pairs={{0,13},{1,14},{2,15},{3,16},{4,17},{5,18},{6,19},{7,20},{8,21},{9,... | collective-permute-start | bytes 98312
  1171.8 65.7 %collective-permute-start.13 = (f32[16,512]{1,0:T(8,128)S(1)}, f32[16,512]{1,0:T(8,128)S(1)}, u32[]{:S(2)}, u32[]{:S(2)}) collective-permute-start(f32[16,512]{1,0:T(8,128)S(1)} %fusion), channel_id=1, source_target_pairs={{0,14},{1,15},{2,16},{3,17},{4,18},{5,19},{6,20},{7,21},{8,22},{9,... | collective-permute-start | bytes 98312
  1184.9 65.7 %collective-permute-start.14 = (f32[16,512]{1,0:T(8,128)S(1)}, f32[16,512]{1,0:T(8,128)S(1)}, u32[]{:S(2)}, u32[]{:S(2)}) collective-permute-start(f32[16,512]{1,0:T(8,128)S(1)} %fusion), channel_id=1, source_target_pairs={{0,15},{1,16},{2,17},{3,18},{4,19},{5,20},{6,21},{7,22},{8,23},{9,... | collective-permute-start | bytes 98312
  1198.0 65.7 %collective-permute-start.15 = (f32[16,512]{1,0:T(8,128)S(1)}, f32[16,512]{1,0:T(8,128)S(1)}, u32[]{:S(2)}, u32[]{:S(2)}) collective-permute-start(f32[16,512]{1,0:T(8,128)S(1)} %fusion), channel_id=1, source_target_pairs={{0,16},{1,17},{2,18},{3,19},{4,20},{5,21},{6,22},{7,23},{8,24},{9,... | collective-permute-start | bytes 98312
  1211.2 65.7 %collective-permute-start.16 = (f32[16,512]{1,0:T(8,128)S(1)}, f32[16,512]{1,0:T(8,128)S(1)}, u32[]{:S(2)}, u32[]{:S(2)}) collective-permute-start(f32[16,512]{1,0:T(8,128)S(1)} %fusion), channel_id=1, source_target_pairs={{0,17},{1,18},{2,19},{3,20},{4,21},{5,22},{6,23},{7,24},{8,25},{9,... | collective-permute-start | bytes 98312
  1224.3 65.7 %collective-permute-start.17 = (f32[16,512]{1,0:T(8,128)S(1)}, f32[16,512]{1,0:T(8,128)S(1)}, u32[]{:S(2)}, u32[]{:S(2)}) collective-permute-start(f32[16,512]{1,0:T(8,128)S(1)} %fusion), channel_id=1, source_target_pairs={{0,18},{1,19},{2,20},{3,21},{4,22},{5,23},{6,24},{7,25},{8,26},{9,... | collective-permute-start | bytes 98312
  1237.5 65.7 %collective-permute-start.18 = (f32[16,512]{1,0:T(8,128)S(1)}, f32[16,512]{1,0:T(8,128)S(1)}, u32[]{:S(2)}, u32[]{:S(2)}) collective-permute-start(f32[16,512]{1,0:T(8,128)S(1)} %fusion), channel_id=1, source_target_pairs={{0,19},{1,20},{2,21},{3,22},{4,23},{5,24},{6,25},{7,26},{8,27},{9,... | collective-permute-start | bytes 98312
  1250.6 65.7 %collective-permute-start.19 = (f32[16,512]{1,0:T(8,128)S(1)}, f32[16,512]{1,0:T(8,128)S(1)}, u32[]{:S(2)}, u32[]{:S(2)}) collective-permute-start(f32[16,512]{1,0:T(8,128)S(1)} %fusion), channel_id=1, source_target_pairs={{0,20},{1,21},{2,22},{3,23},{4,24},{5,25},{6,26},{7,27},{8,28},{9,... | collective-permute-start | bytes 98312
  1263.7 65.7 %collective-permute-start.2 = (f32[16,512]{1,0:T(8,128)S(1)}, f32[16,512]{1,0:T(8,128)S(1)}, u32[]{:S(2)}, u32[]{:S(2)}) collective-permute-start(f32[16,512]{1,0:T(8,128)S(1)} %fusion), channel_id=1, source_target_pairs={{0,3},{1,4},{2,5},{3,6},{4,7},{5,8},{6,9},{7,10},{8,11},{9,12},{10... | collective-permute-start | bytes 98312
  1276.9 65.7 %collective-permute-start.20 = (f32[16,512]{1,0:T(8,128)S(1)}, f32[16,512]{1,0:T(8,128)S(1)}, u32[]{:S(2)}, u32[]{:S(2)}) collective-permute-start(f32[16,512]{1,0:T(8,128)S(1)} %fusion), channel_id=1, source_target_pairs={{0,21},{1,22},{2,23},{3,24},{4,25},{5,26},{6,27},{7,28},{8,29},{9,... | collective-permute-start | bytes 98312
  1290.0 65.7 %collective-permute-start.21 = (f32[16,512]{1,0:T(8,128)S(1)}, f32[16,512]{1,0:T(8,128)S(1)}, u32[]{:S(2)}, u32[]{:S(2)}) collective-permute-start(f32[16,512]{1,0:T(8,128)S(1)} %fusion), channel_id=1, source_target_pairs={{0,22},{1,23},{2,24},{3,25},{4,26},{5,27},{6,28},{7,29},{8,30},{9,... | collective-permute-start | bytes 98312
  1303.2 65.7 %collective-permute-start.22 = (f32[16,512]{1,0:T(8,128)S(1)}, f32[16,512]{1,0:T(8,128)S(1)}, u32[]{:S(2)}, u32[]{:S(2)}) collective-permute-start(f32[16,512]{1,0:T(8,128)S(1)} %fusion), channel_id=1, source_target_pairs={{0,23},{1,24},{2,25},{3,26},{4,27},{5,28},{6,29},{7,30},{8,31},{9,... | collective-permute-start | bytes 98312
  1316.3 65.7 %collective-permute-start.23 = (f32[16,512]{1,0:T(8,128)S(1)}, f32[16,512]{1,0:T(8,128)S(1)}, u32[]{:S(2)}, u32[]{:S(2)}) collective-permute-start(f32[16,512]{1,0:T(8,128)S(1)} %fusion), channel_id=1, source_target_pairs={{0,24},{1,25},{2,26},{3,27},{4,28},{5,29},{6,30},{7,31},{8,32},{9,... | collective-permute-start | bytes 98312
  1329.4 65.7 %collective-permute-start.24 = (f32[16,512]{1,0:T(8,128)S(1)}, f32[16,512]{1,0:T(8,128)S(1)}, u32[]{:S(2)}, u32[]{:S(2)}) collective-permute-start(f32[16,512]{1,0:T(8,128)S(1)} %fusion), channel_id=1, source_target_pairs={{0,25},{1,26},{2,27},{3,28},{4,29},{5,30},{6,31},{7,32},{8,33},{9,... | collective-permute-start | bytes 98312
  1342.6 58.5 %collective-permute-start.25 = (f32[16,512]{1,0:T(8,128)S(1)}, f32[16,512]{1,0:T(8,128)S(1)}, u32[]{:S(2)}, u32[]{:S(2)}) collective-permute-start(f32[16,512]{1,0:T(8,128)S(1)} %fusion), channel_id=1, source_target_pairs={{0,26},{1,27},{2,28},{3,29},{4,30},{5,31},{6,32},{7,33},{8,34},{9,... | collective-permute-start | bytes 98312
  1355.7 56.2 %collective-permute-start.26 = (f32[16,512]{1,0:T(8,128)S(1)}, f32[16,512]{1,0:T(8,128)S(1)}, u32[]{:S(2)}, u32[]{:S(2)}) collective-permute-start(f32[16,512]{1,0:T(8,128)S(1)} %fusion), channel_id=1, source_target_pairs={{0,27},{1,28},{2,29},{3,30},{4,31},{5,32},{6,33},{7,34},{8,35},{9,... | collective-permute-start | bytes 98312
  1368.9 48.7 %collective-permute-start.27 = (f32[16,512]{1,0:T(8,128)S(1)}, f32[16,512]{1,0:T(8,128)S(1)}, u32[]{:S(2)}, u32[]{:S(2)}) collective-permute-start(f32[16,512]{1,0:T(8,128)S(1)} %fusion), channel_id=1, source_target_pairs={{0,28},{1,29},{2,30},{3,31},{4,32},{5,33},{6,34},{7,35},{8,36},{9,... | collective-permute-start | bytes 98312
  1382.0 39.6 %collective-permute-start.28 = (f32[16,512]{1,0:T(8,128)S(1)}, f32[16,512]{1,0:T(8,128)S(1)}, u32[]{:S(2)}, u32[]{:S(2)}) collective-permute-start(f32[16,512]{1,0:T(8,128)S(1)} %fusion), channel_id=1, source_target_pairs={{0,29},{1,30},{2,31},{3,32},{4,33},{5,34},{6,35},{7,36},{8,37},{9,... | collective-permute-start | bytes 98312
  1431.3 35.2 %collective-permute-start.37 = (f32[16,512]{1,0:T(8,128)S(1)}, f32[16,512]{1,0:T(8,128)S(1)}, u32[]{:S(2)}, u32[]{:S(2)}) collective-permute-start(f32[16,512]{1,0:T(8,128)S(1)} %fusion), channel_id=1, source_target_pairs={{0,38},{1,39},{2,40},{3,41},{4,42},{5,43},{6,44},{7,45},{8,46},{9,... | collective-permute-start | bytes 98312
  1433.2 35.8 %collective-permute-start.38 = (f32[16,512]{1,0:T(8,128)S(1)}, f32[16,512]{1,0:T(8,128)S(1)}, u32[]{:S(2)}, u32[]{:S(2)}) collective-permute-start(f32[16,512]{1,0:T(8,128)S(1)} %fusion), channel_id=1, source_target_pairs={{0,39},{1,40},{2,41},{3,42},{4,43},{5,44},{6,45},{7,46},{8,47},{9,... | collective-permute-start | bytes 98312
  1435.2 35.8 %collective-permute-start.39 = (f32[16,512]{1,0:T(8,128)S(1)}, f32[16,512]{1,0:T(8,128)S(1)}, u32[]{:S(2)}, u32[]{:S(2)}) collective-permute-start(f32[16,512]{1,0:T(8,128)S(1)} %fusion), channel_id=1, source_target_pairs={{0,40},{1,41},{2,42},{3,43},{4,44},{5,45},{6,46},{7,47},{8,48},{9,... | collective-permute-start | bytes 98312
  1437.1 36.1 %collective-permute-start.4 = (f32[16,512]{1,0:T(8,128)S(1)}, f32[16,512]{1,0:T(8,128)S(1)}, u32[]{:S(2)}, u32[]{:S(2)}) collective-permute-start(f32[16,512]{1,0:T(8,128)S(1)} %fusion), channel_id=1, source_target_pairs={{0,5},{1,6},{2,7},{3,8},{4,9},{5,10},{6,11},{7,12},{8,13},{9,14},{... | collective-permute-start | bytes 98312
  1485.3 33.3 %collective-permute-start.5 = (f32[16,512]{1,0:T(8,128)S(1)}, f32[16,512]{1,0:T(8,128)S(1)}, u32[]{:S(2)}, u32[]{:S(2)}) collective-permute-start(f32[16,512]{1,0:T(8,128)S(1)} %fusion), channel_id=1, source_target_pairs={{0,6},{1,7},{2,8},{3,9},{4,10},{5,11},{6,12},{7,13},{8,14},{9,15},... | collective-permute-start | bytes 98312
  1530.3 40.4 %collective-permute-start.6 = (f32[16,512]{1,0:T(8,128)S(1)}, f32[16,512]{1,0:T(8,128)S(1)}, u32[]{:S(2)}, u32[]{:S(2)}) collective-permute-start(f32[16,512]{1,0:T(8,128)S(1)} %fusion), channel_id=1, source_target_pairs={{0,7},{1,8},{2,9},{3,10},{4,11},{5,12},{6,13},{7,14},{8,15},{9,16}... | collective-permute-start | bytes 98312
  1547.6 36.2 %collective-permute-start.60 = (f32[16,512]{1,0:T(8,128)S(1)}, f32[16,512]{1,0:T(8,128)S(1)}, u32[]{:S(2)}, u32[]{:S(2)}) collective-permute-start(f32[16,512]{1,0:T(8,128)S(1)} %fusion), channel_id=1, source_target_pairs={{0,61},{1,62},{2,63},{3,64},{4,65},{5,66},{6,67},{7,68},{8,69},{9,... | collective-permute-start | bytes 98312
  1554.1 43.2 %collective-permute-start.61 = (f32[16,512]{1,0:T(8,128)S(1)}, f32[16,512]{1,0:T(8,128)S(1)}, u32[]{:S(2)}, u32[]{:S(2)}) collective-permute-start(f32[16,512]{1,0:T(8,128)S(1)} %fusion), channel_id=1, source_target_pairs={{0,62},{1,63},{2,64},{3,65},{4,66},{5,67},{6,68},{7,69},{8,70},{9,... | collective-permute-start | bytes 98312
  1556.1 41.3 %collective-permute-start.62 = (f32[16,512]{1,0:T(8,128)S(1)}, f32[16,512]{1,0:T(8,128)S(1)}, u32[]{:S(2)}, u32[]{:S(2)}) collective-permute-start(f32[16,512]{1,0:T(8,128)S(1)} %fusion), channel_id=1, source_target_pairs={{0,63},{1,64},{2,65},{3,66},{4,67},{5,68},{6,69},{7,70},{8,71},{9,... | collective-permute-start | bytes 98312
  1558.0 39.3 %collective-permute-start.7 = (f32[16,512]{1,0:T(8,128)S(1)}, f32[16,512]{1,0:T(8,128)S(1)}, u32[]{:S(2)}, u32[]{:S(2)}) collective-permute-start(f32[16,512]{1,0:T(8,128)S(1)} %fusion), channel_id=1, source_target_pairs={{0,8},{1,9},{2,10},{3,11},{4,12},{5,13},{6,14},{7,15},{8,16},{9,17... | collective-permute-start | bytes 98312
  (60 other events, 2292.8 us)
where the time goes:
time: 1630 us
  blocking collectives  954 us (59%)
  starting transfers between devices  565 us (35%)
  other arithmetic  59.6 us (4%)
  local copies, waits for them, and re-layouts  26 us (2%)
    unnamed x1, blocking collectives  647 us
    unnamed x64, starting transfers between devices  565 us
    all_gather x1, blocking collectives, on_device(): all_points = lax.all_gather(local_points, ('ga', 'orb'), axis=1, tiled=True)  307 us
    convert_element_type x6, other arithmetic, add_panel(): jnp.cos(angle).astype(jnp.bfloat16)  55.8 us
  transfers between devices with their start and end apart: 64, of which 1 were waited for; matrix products, arithmetic and copies ran while one was open for 0% of the time, Pallas kernels for 0%

commit v1 on v0

--- a/solution.py
+++ b/solution.py
@@ -48,7 +48,12 @@
     coefficients, triples, elec_pos, ion_pos, assignment, rotation, quad_table, inverse_rows
 ):
     local_points = point_coords(elec_pos, ion_pos, assignment, rotation, quad_table)
-    all_points = lax.all_gather(local_points, ("ga", "orb"), axis=1, tiled=True)
+    all_points = jnp.concatenate(
+        lax.all_to_all(
+            jnp.stack([local_points] * lax.axis_size(("ga", "orb"))), ("ga", "orb"), 0, 0
+        ),
+        axis=1,
+    )
     electrons = inverse_rows.shape[0]
     values = lax.psum_scatter(
         phase_values(all_points, triples, coefficients),

time: 1630 us -> 1310 us (0.80)
  blocking collectives: 954 us -> 610 us
    all_gather x1 -> x0, blocking collectives: 307 us -> none  [on_device(): all_points = lax.all_gather(local_points, ('ga', 'orb'), axis=1, tiled=True)]
    unnamed x1, blocking collectives: 647 us -> 610 us
  transfers between devices with their start and end apart: 64 -> 65, of which waited for: 1 -> 2; matrix products, arithmetic and copies ran while one was open for 0% -> 0% of each run, Pallas kernels for 0% -> 0%
where the time goes in v1:
time: 1310 us
  blocking collectives  610 us (47%)
  starting transfers between devices  572 us (44%)
  other arithmetic  59.6 us (5%)
  local copies, waits for them, and re-layouts  26.9 us (2%)
  waiting for transfers between devices  22.7 us (2%)
  matrix products  14.3 us (1%)
    unnamed x1, blocking collectives  610 us
    unnamed x64, starting transfers between devices  558 us
    convert_element_type x6, other arithmetic, add_panel(): jnp.cos(angle).astype(jnp.bfloat16)  55.8 us
  transfers between devices with their start and end apart: 65, of which 2 were waited for; matrix products, arithmetic and copies ran while one was open for 0% of the time, Pallas kernels for 0%

profile of v1, /device:TPU:192, one launch (start us, length us, event | category | flops | bytes accessed | tf_op | source)
XLA Modules:
  0.0 1309.0 jit_solution(4269359673316474000)
XLA Ops:
  6.0 13.5 %all-to-all-start = ((f32[256,3,12]{2,1,0:T(4,128)}), f32[256,3,12]{2,1,0:T(4,128)S(1)}, u32[]{:S(2)}, u32[]{:S(2)}) async-start(f32[256,3,12]{2,1,0:T(4,128)} %stack.3), calls=%async_computation | async-start | bytes 1048576 | tf_op jit(solution)/shard_map/all_to_all | solution.py:52
  20.2 15.6 %all-to-all-done = f32[256,3,12]{2,1,0:T(4,128)S(1)} async-done(((f32[256,3,12]{2,1,0:T(4,128)}), f32[256,3,12]{2,1,0:T(4,128)S(1)}, u32[]{:S(2)}, u32[]{:S(2)}) %all-to-all-start) | async-done | bytes 36896 | tf_op jit(solution)/shard_map/all_to_all | solution.py:52
  36.1 70.7 %while.16 = (s32[]{:T(128)}, f32[6,512,512]{2,1,0:T(8,128)}, f32[6,3,512]{2,0,1:T(8,128)S(1)}, f32[3,1152]{1,0:T(4,128)S(1)}, bf16[2,1152,512]{2,1,0:T(8,128)(2,1)}, /*index=5*/s32[]{:T(128)}, s32[]{:T(128)}, s32[]{}, s32[]{}) while((s32[]{:T(128)}, f32[6,512,512]{2,1,0:T(8,128)}, f32[6,3,512]{2,0,1:T(8,128)S(1)}, f32[3,1152]{1,0:T(4,128)S(1)}, ...), condition=%wide.region_2.3_spmd, body=%wide.region_1.2_spmd.sunk | while | flops 1216806912 | bytes 17624220 | solution.py:44
  106.8 610.4 %fusion = f32[16,512]{1,0:T(8,128)S(1)} fusion(f32[3072,512]{1,0:T(8,128)} %bitcast.36), kind=kCustom, calls=%all-reduce-scatter | all-reduce-scatter fusion | flops 2097153 | bytes 6324224
  717.2 85.6 %collective-permute-start = (f32[16,512]{1,0:T(8,128)S(1)}, f32[16,512]{1,0:T(8,128)S(1)}, u32[]{:S(2)}, u32[]{:S(2)}) collective-permute-start(f32[16,512]{1,0:T(8,128)S(1)} %fusion), channel_id=1, source_target_pairs={{0,1},{1,2},{2,3},{3,4},{4,5},{5,6},{6,7},{7,8},{8,9},{9,10},{10,1... | collective-permute-start | bytes 98312
  802.8 13.1 %collective-permute-start.1 = (f32[16,512]{1,0:T(8,128)S(1)}, f32[16,512]{1,0:T(8,128)S(1)}, u32[]{:S(2)}, u32[]{:S(2)}) collective-permute-start(f32[16,512]{1,0:T(8,128)S(1)} %fusion), channel_id=1, source_target_pairs={{0,2},{1,3},{2,4},{3,5},{4,6},{5,7},{6,8},{7,9},{8,10},{9,11},{10,... | collective-permute-start | bytes 98312
  816.0 13.1 %collective-permute-start.10 = (f32[16,512]{1,0:T(8,128)S(1)}, f32[16,512]{1,0:T(8,128)S(1)}, u32[]{:S(2)}, u32[]{:S(2)}) collective-permute-start(f32[16,512]{1,0:T(8,128)S(1)} %fusion), channel_id=1, source_target_pairs={{0,11},{1,12},{2,13},{3,14},{4,15},{5,16},{6,17},{7,18},{8,19},{9,... | collective-permute-start | bytes 98312
  830.4 14.8 %collective-permute-start.11 = (f32[16,512]{1,0:T(8,128)S(1)}, f32[16,512]{1,0:T(8,128)S(1)}, u32[]{:S(2)}, u32[]{:S(2)}) collective-permute-start(f32[16,512]{1,0:T(8,128)S(1)} %fusion), channel_id=1, source_target_pairs={{0,12},{1,13},{2,14},{3,15},{4,16},{5,17},{6,18},{7,19},{8,20},{9,... | collective-permute-start | bytes 98312
  845.3 13.1 %collective-permute-start.12 = (f32[16,512]{1,0:T(8,128)S(1)}, f32[16,512]{1,0:T(8,128)S(1)}, u32[]{:S(2)}, u32[]{:S(2)}) collective-permute-start(f32[16,512]{1,0:T(8,128)S(1)} %fusion), channel_id=1, source_target_pairs={{0,13},{1,14},{2,15},{3,16},{4,17},{5,18},{6,19},{7,20},{8,21},{9,... | collective-permute-start | bytes 98312
  858.4 13.1 %collective-permute-start.13 = (f32[16,512]{1,0:T(8,128)S(1)}, f32[16,512]{1,0:T(8,128)S(1)}, u32[]{:S(2)}, u32[]{:S(2)}) collective-permute-start(f32[16,512]{1,0:T(8,128)S(1)} %fusion), channel_id=1, source_target_pairs={{0,14},{1,15},{2,16},{3,17},{4,18},{5,19},{6,20},{7,21},{8,22},{9,... | collective-permute-start | bytes 98312
  871.5 13.1 %collective-permute-start.14 = (f32[16,512]{1,0:T(8,128)S(1)}, f32[16,512]{1,0:T(8,128)S(1)}, u32[]{:S(2)}, u32[]{:S(2)}) collective-permute-start(f32[16,512]{1,0:T(8,128)S(1)} %fusion), channel_id=1, source_target_pairs={{0,15},{1,16},{2,17},{3,18},{4,19},{5,20},{6,21},{7,22},{8,23},{9,... | collective-permute-start | bytes 98312
  884.7 13.1 %collective-permute-start.15 = (f32[16,512]{1,0:T(8,128)S(1)}, f32[16,512]{1,0:T(8,128)S(1)}, u32[]{:S(2)}, u32[]{:S(2)}) collective-permute-start(f32[16,512]{1,0:T(8,128)S(1)} %fusion), channel_id=1, source_target_pairs={{0,16},{1,17},{2,18},{3,19},{4,20},{5,21},{6,22},{7,23},{8,24},{9,... | collective-permute-start | bytes 98312
  897.8 13.1 %collective-permute-start.16 = (f32[16,512]{1,0:T(8,128)S(1)}, f32[16,512]{1,0:T(8,128)S(1)}, u32[]{:S(2)}, u32[]{:S(2)}) collective-permute-start(f32[16,512]{1,0:T(8,128)S(1)} %fusion), channel_id=1, source_target_pairs={{0,17},{1,18},{2,19},{3,20},{4,21},{5,22},{6,23},{7,24},{8,25},{9,... | collective-permute-start | bytes 98312
  911.0 13.1 %collective-permute-start.17 = (f32[16,512]{1,0:T(8,128)S(1)}, f32[16,512]{1,0:T(8,128)S(1)}, u32[]{:S(2)}, u32[]{:S(2)}) collective-permute-start(f32[16,512]{1,0:T(8,128)S(1)} %fusion), channel_id=1, source_target_pairs={{0,18},{1,19},{2,20},{3,21},{4,22},{5,23},{6,24},{7,25},{8,26},{9,... | collective-permute-start | bytes 98312
  924.1 13.1 %collective-permute-start.18 = (f32[16,512]{1,0:T(8,128)S(1)}, f32[16,512]{1,0:T(8,128)S(1)}, u32[]{:S(2)}, u32[]{:S(2)}) collective-permute-start(f32[16,512]{1,0:T(8,128)S(1)} %fusion), channel_id=1, source_target_pairs={{0,19},{1,20},{2,21},{3,22},{4,23},{5,24},{6,25},{7,26},{8,27},{9,... | collective-permute-start | bytes 98312
  937.2 13.1 %collective-permute-start.19 = (f32[16,512]{1,0:T(8,128)S(1)}, f32[16,512]{1,0:T(8,128)S(1)}, u32[]{:S(2)}, u32[]{:S(2)}) collective-permute-start(f32[16,512]{1,0:T(8,128)S(1)} %fusion), channel_id=1, source_target_pairs={{0,20},{1,21},{2,22},{3,23},{4,24},{5,25},{6,26},{7,27},{8,28},{9,... | collective-permute-start | bytes 98312
  950.4 13.1 %collective-permute-start.2 = (f32[16,512]{1,0:T(8,128)S(1)}, f32[16,512]{1,0:T(8,128)S(1)}, u32[]{:S(2)}, u32[]{:S(2)}) collective-permute-start(f32[16,512]{1,0:T(8,128)S(1)} %fusion), channel_id=1, source_target_pairs={{0,3},{1,4},{2,5},{3,6},{4,7},{5,8},{6,9},{7,10},{8,11},{9,12},{10... | collective-permute-start | bytes 98312
  963.5 13.1 %collective-permute-start.20 = (f32[16,512]{1,0:T(8,128)S(1)}, f32[16,512]{1,0:T(8,128)S(1)}, u32[]{:S(2)}, u32[]{:S(2)}) collective-permute-start(f32[16,512]{1,0:T(8,128)S(1)} %fusion), channel_id=1, source_target_pairs={{0,21},{1,22},{2,23},{3,24},{4,25},{5,26},{6,27},{7,28},{8,29},{9,... | collective-permute-start | bytes 98312
  976.7 13.1 %collective-permute-start.21 = (f32[16,512]{1,0:T(8,128)S(1)}, f32[16,512]{1,0:T(8,128)S(1)}, u32[]{:S(2)}, u32[]{:S(2)}) collective-permute-start(f32[16,512]{1,0:T(8,128)S(1)} %fusion), channel_id=1, source_target_pairs={{0,22},{1,23},{2,24},{3,25},{4,26},{5,27},{6,28},{7,29},{8,30},{9,... | collective-permute-start | bytes 98312
  989.8 13.1 %collective-permute-start.22 = (f32[16,512]{1,0:T(8,128)S(1)}, f32[16,512]{1,0:T(8,128)S(1)}, u32[]{:S(2)}, u32[]{:S(2)}) collective-permute-start(f32[16,512]{1,0:T(8,128)S(1)} %fusion), channel_id=1, source_target_pairs={{0,23},{1,24},{2,25},{3,26},{4,27},{5,28},{6,29},{7,30},{8,31},{9,... | collective-permute-start | bytes 98312
  1002.9 13.1 %collective-permute-start.23 = (f32[16,512]{1,0:T(8,128)S(1)}, f32[16,512]{1,0:T(8,128)S(1)}, u32[]{:S(2)}, u32[]{:S(2)}) collective-permute-start(f32[16,512]{1,0:T(8,128)S(1)} %fusion), channel_id=1, source_target_pairs={{0,24},{1,25},{2,26},{3,27},{4,28},{5,29},{6,30},{7,31},{8,32},{9,... | collective-permute-start | bytes 98312
  1016.1 13.1 %collective-permute-start.24 = (f32[16,512]{1,0:T(8,128)S(1)}, f32[16,512]{1,0:T(8,128)S(1)}, u32[]{:S(2)}, u32[]{:S(2)}) collective-permute-start(f32[16,512]{1,0:T(8,128)S(1)} %fusion), channel_id=1, source_target_pairs={{0,25},{1,26},{2,27},{3,28},{4,29},{5,30},{6,31},{7,32},{8,33},{9,... | collective-permute-start | bytes 98312
  1029.2 13.1 %collective-permute-start.25 = (f32[16,512]{1,0:T(8,128)S(1)}, f32[16,512]{1,0:T(8,128)S(1)}, u32[]{:S(2)}, u32[]{:S(2)}) collective-permute-start(f32[16,512]{1,0:T(8,128)S(1)} %fusion), channel_id=1, source_target_pairs={{0,26},{1,27},{2,28},{3,29},{4,30},{5,31},{6,32},{7,33},{8,34},{9,... | collective-permute-start | bytes 98312
  1042.4 13.1 %collective-permute-start.26 = (f32[16,512]{1,0:T(8,128)S(1)}, f32[16,512]{1,0:T(8,128)S(1)}, u32[]{:S(2)}, u32[]{:S(2)}) collective-permute-start(f32[16,512]{1,0:T(8,128)S(1)} %fusion), channel_id=1, source_target_pairs={{0,27},{1,28},{2,29},{3,30},{4,31},{5,32},{6,33},{7,34},{8,35},{9,... | collective-permute-start | bytes 98312
  1055.5 13.1 %collective-permute-start.27 = (f32[16,512]{1,0:T(8,128)S(1)}, f32[16,512]{1,0:T(8,128)S(1)}, u32[]{:S(2)}, u32[]{:S(2)}) collective-permute-start(f32[16,512]{1,0:T(8,128)S(1)} %fusion), channel_id=1, source_target_pairs={{0,28},{1,29},{2,30},{3,31},{4,32},{5,33},{6,34},{7,35},{8,36},{9,... | collective-permute-start | bytes 98312
  1078.5 12.9 collective-permute-start.3
  1116.6 24.4 %collective-permute-start.4 = (f32[16,512]{1,0:T(8,128)S(1)}, f32[16,512]{1,0:T(8,128)S(1)}, u32[]{:S(2)}, u32[]{:S(2)}) collective-permute-start(f32[16,512]{1,0:T(8,128)S(1)} %fusion), channel_id=1, source_target_pairs={{0,5},{1,6},{2,7},{3,8},{4,9},{5,10},{6,11},{7,12},{8,13},{9,14},{... | collective-permute-start | bytes 98312
  1164.8 20.8 %collective-permute-start.5 = (f32[16,512]{1,0:T(8,128)S(1)}, f32[16,512]{1,0:T(8,128)S(1)}, u32[]{:S(2)}, u32[]{:S(2)}) collective-permute-start(f32[16,512]{1,0:T(8,128)S(1)} %fusion), channel_id=1, source_target_pairs={{0,6},{1,7},{2,8},{3,9},{4,10},{5,11},{6,12},{7,13},{8,14},{9,15},... | collective-permute-start | bytes 98312
  1209.8 17.3 %collective-permute-start.6 = (f32[16,512]{1,0:T(8,128)S(1)}, f32[16,512]{1,0:T(8,128)S(1)}, u32[]{:S(2)}, u32[]{:S(2)}) collective-permute-start(f32[16,512]{1,0:T(8,128)S(1)} %fusion), channel_id=1, source_target_pairs={{0,7},{1,8},{2,9},{3,10},{4,11},{5,12},{6,13},{7,14},{8,15},{9,16}... | collective-permute-start | bytes 98312
  1250.2 13.1 %collective-permute-start.8 = (f32[16,512]{1,0:T(8,128)S(1)}, f32[16,512]{1,0:T(8,128)S(1)}, u32[]{:S(2)}, u32[]{:S(2)}) collective-permute-start(f32[16,512]{1,0:T(8,128)S(1)} %fusion), channel_id=1, source_target_pairs={{0,9},{1,10},{2,11},{3,12},{4,13},{5,14},{6,15},{7,16},{8,17},{9,1... | collective-permute-start | bytes 98312
  1263.3 13.3 %collective-permute-start.9 = (f32[16,512]{1,0:T(8,128)S(1)}, f32[16,512]{1,0:T(8,128)}, u32[]{:S(2)}, u32[]{:S(2)}) collective-permute-start(f32[16,512]{1,0:T(8,128)S(1)} %fusion), channel_id=1, source_target_pairs={{0,10},{1,11},{2,12},{3,13},{4,14},{5,15},{6,16},{7,17},{8,18},{9,... | collective-permute-start | bytes 98312
  1285.0 23.3 %concatenate.6 = f32[1036,512]{1,0:T(8,128)S(1)} concatenate(f32[12,512]{1,0:T(8,128)S(1)} %collective-permute-done.63, f32[16,512]{1,0:T(8,128)} %copy-done.18, f32[16,512]{1,0:T(8,128)} %copy-done.17, f32[16,512]{1,0:T(8,128)} %copy-done.16, f32[16,512]{1,0:T(8,128)} %copy-done.14, f32[16,512]{1,0:T(8,128)} %copy-done.13, f32[16,512]{1,0:T(8,128)} %copy-done.12, ...), dimensions={0} | concatenate | bytes 4243456
  (192 shorter events, 191.1 us)
Async XLA Ops:
  717.2 141.2 %collective-permute-start = (f32[16,512]{1,0:T(8,128)S(1)}, f32[16,512]{1,0:T(8,128)S(1)}, u32[]{:S(2)}, u32[]{:S(2)}) collective-permute-start(f32[16,512]{1,0:T(8,128)S(1)} %fusion), channel_id=1, source_target_pairs={{0,1},{1,2},{2,3},{3,4},{4,5},{5,6},{6,7},{7,8},{8,9},{9,10},{10,1... | collective-permute-start | bytes 98312
  802.8 68.7 %collective-permute-start.1 = (f32[16,512]{1,0:T(8,128)S(1)}, f32[16,512]{1,0:T(8,128)S(1)}, u32[]{:S(2)}, u32[]{:S(2)}) collective-permute-start(f32[16,512]{1,0:T(8,128)S(1)} %fusion), channel_id=1, source_target_pairs={{0,2},{1,3},{2,4},{3,5},{4,6},{5,7},{6,8},{7,9},{8,10},{9,11},{10,... | collective-permute-start | bytes 98312
  816.0 68.7 %collective-permute-start.10 = (f32[16,512]{1,0:T(8,128)S(1)}, f32[16,512]{1,0:T(8,128)S(1)}, u32[]{:S(2)}, u32[]{:S(2)}) collective-permute-start(f32[16,512]{1,0:T(8,128)S(1)} %fusion), channel_id=1, source_target_pairs={{0,11},{1,12},{2,13},{3,14},{4,15},{5,16},{6,17},{7,18},{8,19},{9,... | collective-permute-start | bytes 98312
  830.4 67.4 %collective-permute-start.11 = (f32[16,512]{1,0:T(8,128)S(1)}, f32[16,512]{1,0:T(8,128)S(1)}, u32[]{:S(2)}, u32[]{:S(2)}) collective-permute-start(f32[16,512]{1,0:T(8,128)S(1)} %fusion), channel_id=1, source_target_pairs={{0,12},{1,13},{2,14},{3,15},{4,16},{5,17},{6,18},{7,19},{8,20},{9,... | collective-permute-start | bytes 98312
  845.3 65.7 %collective-permute-start.12 = (f32[16,512]{1,0:T(8,128)S(1)}, f32[16,512]{1,0:T(8,128)S(1)}, u32[]{:S(2)}, u32[]{:S(2)}) collective-permute-start(f32[16,512]{1,0:T(8,128)S(1)} %fusion), channel_id=1, source_target_pairs={{0,13},{1,14},{2,15},{3,16},{4,17},{5,18},{6,19},{7,20},{8,21},{9,... | collective-permute-start | bytes 98312
  858.4 65.7 %collective-permute-start.13 = (f32[16,512]{1,0:T(8,128)S(1)}, f32[16,512]{1,0:T(8,128)S(1)}, u32[]{:S(2)}, u32[]{:S(2)}) collective-permute-start(f32[16,512]{1,0:T(8,128)S(1)} %fusion), channel_id=1, source_target_pairs={{0,14},{1,15},{2,16},{3,17},{4,18},{5,19},{6,20},{7,21},{8,22},{9,... | collective-permute-start | bytes 98312
  871.5 65.7 %collective-permute-start.14 = (f32[16,512]{1,0:T(8,128)S(1)}, f32[16,512]{1,0:T(8,128)S(1)}, u32[]{:S(2)}, u32[]{:S(2)}) collective-permute-start(f32[16,512]{1,0:T(8,128)S(1)} %fusion), channel_id=1, source_target_pairs={{0,15},{1,16},{2,17},{3,18},{4,19},{5,20},{6,21},{7,22},{8,23},{9,... | collective-permute-start | bytes 98312
  884.7 65.7 %collective-permute-start.15 = (f32[16,512]{1,0:T(8,128)S(1)}, f32[16,512]{1,0:T(8,128)S(1)}, u32[]{:S(2)}, u32[]{:S(2)}) collective-permute-start(f32[16,512]{1,0:T(8,128)S(1)} %fusion), channel_id=1, source_target_pairs={{0,16},{1,17},{2,18},{3,19},{4,20},{5,21},{6,22},{7,23},{8,24},{9,... | collective-permute-start | bytes 98312
  897.8 65.7 %collective-permute-start.16 = (f32[16,512]{1,0:T(8,128)S(1)}, f32[16,512]{1,0:T(8,128)S(1)}, u32[]{:S(2)}, u32[]{:S(2)}) collective-permute-start(f32[16,512]{1,0:T(8,128)S(1)} %fusion), channel_id=1, source_target_pairs={{0,17},{1,18},{2,19},{3,20},{4,21},{5,22},{6,23},{7,24},{8,25},{9,... | collective-permute-start | bytes 98312
  911.0 65.7 %collective-permute-start.17 = (f32[16,512]{1,0:T(8,128)S(1)}, f32[16,512]{1,0:T(8,128)S(1)}, u32[]{:S(2)}, u32[]{:S(2)}) collective-permute-start(f32[16,512]{1,0:T(8,128)S(1)} %fusion), channel_id=1, source_target_pairs={{0,18},{1,19},{2,20},{3,21},{4,22},{5,23},{6,24},{7,25},{8,26},{9,... | collective-permute-start | bytes 98312
  924.1 65.7 %collective-permute-start.18 = (f32[16,512]{1,0:T(8,128)S(1)}, f32[16,512]{1,0:T(8,128)S(1)}, u32[]{:S(2)}, u32[]{:S(2)}) collective-permute-start(f32[16,512]{1,0:T(8,128)S(1)} %fusion), channel_id=1, source_target_pairs={{0,19},{1,20},{2,21},{3,22},{4,23},{5,24},{6,25},{7,26},{8,27},{9,... | collective-permute-start | bytes 98312
  937.2 65.7 %collective-permute-start.19 = (f32[16,512]{1,0:T(8,128)S(1)}, f32[16,512]{1,0:T(8,128)S(1)}, u32[]{:S(2)}, u32[]{:S(2)}) collective-permute-start(f32[16,512]{1,0:T(8,128)S(1)} %fusion), channel_id=1, source_target_pairs={{0,20},{1,21},{2,22},{3,23},{4,24},{5,25},{6,26},{7,27},{8,28},{9,... | collective-permute-start | bytes 98312
  950.4 65.7 %collective-permute-start.2 = (f32[16,512]{1,0:T(8,128)S(1)}, f32[16,512]{1,0:T(8,128)S(1)}, u32[]{:S(2)}, u32[]{:S(2)}) collective-permute-start(f32[16,512]{1,0:T(8,128)S(1)} %fusion), channel_id=1, source_target_pairs={{0,3},{1,4},{2,5},{3,6},{4,7},{5,8},{6,9},{7,10},{8,11},{9,12},{10... | collective-permute-start | bytes 98312
  963.5 65.7 %collective-permute-start.20 = (f32[16,512]{1,0:T(8,128)S(1)}, f32[16,512]{1,0:T(8,128)S(1)}, u32[]{:S(2)}, u32[]{:S(2)}) collective-permute-start(f32[16,512]{1,0:T(8,128)S(1)} %fusion), channel_id=1, source_target_pairs={{0,21},{1,22},{2,23},{3,24},{4,25},{5,26},{6,27},{7,28},{8,29},{9,... | collective-permute-start | bytes 98312
  976.7 65.7 %collective-permute-start.21 = (f32[16,512]{1,0:T(8,128)S(1)}, f32[16,512]{1,0:T(8,128)S(1)}, u32[]{:S(2)}, u32[]{:S(2)}) collective-permute-start(f32[16,512]{1,0:T(8,128)S(1)} %fusion), channel_id=1, source_target_pairs={{0,22},{1,23},{2,24},{3,25},{4,26},{5,27},{6,28},{7,29},{8,30},{9,... | collective-permute-start | bytes 98312
  989.8 65.7 %collective-permute-start.22 = (f32[16,512]{1,0:T(8,128)S(1)}, f32[16,512]{1,0:T(8,128)S(1)}, u32[]{:S(2)}, u32[]{:S(2)}) collective-permute-start(f32[16,512]{1,0:T(8,128)S(1)} %fusion), channel_id=1, source_target_pairs={{0,23},{1,24},{2,25},{3,26},{4,27},{5,28},{6,29},{7,30},{8,31},{9,... | collective-permute-start | bytes 98312
  1002.9 65.7 %collective-permute-start.23 = (f32[16,512]{1,0:T(8,128)S(1)}, f32[16,512]{1,0:T(8,128)S(1)}, u32[]{:S(2)}, u32[]{:S(2)}) collective-permute-start(f32[16,512]{1,0:T(8,128)S(1)} %fusion), channel_id=1, source_target_pairs={{0,24},{1,25},{2,26},{3,27},{4,28},{5,29},{6,30},{7,31},{8,32},{9,... | collective-permute-start | bytes 98312
  1016.1 58.5 %collective-permute-start.24 = (f32[16,512]{1,0:T(8,128)S(1)}, f32[16,512]{1,0:T(8,128)S(1)}, u32[]{:S(2)}, u32[]{:S(2)}) collective-permute-start(f32[16,512]{1,0:T(8,128)S(1)} %fusion), channel_id=1, source_target_pairs={{0,25},{1,26},{2,27},{3,28},{4,29},{5,30},{6,31},{7,32},{8,33},{9,... | collective-permute-start | bytes 98312
  1029.2 49.3 %collective-permute-start.25 = (f32[16,512]{1,0:T(8,128)S(1)}, f32[16,512]{1,0:T(8,128)S(1)}, u32[]{:S(2)}, u32[]{:S(2)}) collective-permute-start(f32[16,512]{1,0:T(8,128)S(1)} %fusion), channel_id=1, source_target_pairs={{0,26},{1,27},{2,28},{3,29},{4,30},{5,31},{6,32},{7,33},{8,34},{9,... | collective-permute-start | bytes 98312
  1042.4 49.0 %collective-permute-start.26 = (f32[16,512]{1,0:T(8,128)S(1)}, f32[16,512]{1,0:T(8,128)S(1)}, u32[]{:S(2)}, u32[]{:S(2)}) collective-permute-start(f32[16,512]{1,0:T(8,128)S(1)} %fusion), channel_id=1, source_target_pairs={{0,27},{1,28},{2,29},{3,30},{4,31},{5,32},{6,33},{7,34},{8,35},{9,... | collective-permute-start | bytes 98312
  1055.5 41.6 %collective-permute-start.27 = (f32[16,512]{1,0:T(8,128)S(1)}, f32[16,512]{1,0:T(8,128)S(1)}, u32[]{:S(2)}, u32[]{:S(2)}) collective-permute-start(f32[16,512]{1,0:T(8,128)S(1)} %fusion), channel_id=1, source_target_pairs={{0,28},{1,29},{2,30},{3,31},{4,32},{5,33},{6,34},{7,35},{8,36},{9,... | collective-permute-start | bytes 98312
  1110.7 35.2 %collective-permute-start.37 = (f32[16,512]{1,0:T(8,128)S(1)}, f32[16,512]{1,0:T(8,128)S(1)}, u32[]{:S(2)}, u32[]{:S(2)}) collective-permute-start(f32[16,512]{1,0:T(8,128)S(1)} %fusion), channel_id=1, source_target_pairs={{0,38},{1,39},{2,40},{3,41},{4,42},{5,43},{6,44},{7,45},{8,46},{9,... | collective-permute-start | bytes 98312
  1112.7 35.8 %collective-permute-start.38 = (f32[16,512]{1,0:T(8,128)S(1)}, f32[16,512]{1,0:T(8,128)S(1)}, u32[]{:S(2)}, u32[]{:S(2)}) collective-permute-start(f32[16,512]{1,0:T(8,128)S(1)} %fusion), channel_id=1, source_target_pairs={{0,39},{1,40},{2,41},{3,42},{4,43},{5,44},{6,45},{7,46},{8,47},{9,... | collective-permute-start | bytes 98312
  1114.6 35.8 %collective-permute-start.39 = (f32[16,512]{1,0:T(8,128)S(1)}, f32[16,512]{1,0:T(8,128)S(1)}, u32[]{:S(2)}, u32[]{:S(2)}) collective-permute-start(f32[16,512]{1,0:T(8,128)S(1)} %fusion), channel_id=1, source_target_pairs={{0,40},{1,41},{2,42},{3,43},{4,44},{5,45},{6,46},{7,47},{8,48},{9,... | collective-permute-start | bytes 98312
  1116.6 36.1 %collective-permute-start.4 = (f32[16,512]{1,0:T(8,128)S(1)}, f32[16,512]{1,0:T(8,128)S(1)}, u32[]{:S(2)}, u32[]{:S(2)}) collective-permute-start(f32[16,512]{1,0:T(8,128)S(1)} %fusion), channel_id=1, source_target_pairs={{0,5},{1,6},{2,7},{3,8},{4,9},{5,10},{6,11},{7,12},{8,13},{9,14},{... | collective-permute-start | bytes 98312
  1162.9 33.3 %collective-permute-start.49 = (f32[16,512]{1,0:T(8,128)S(1)}, f32[16,512]{1,0:T(8,128)S(1)}, u32[]{:S(2)}, u32[]{:S(2)}) collective-permute-start(f32[16,512]{1,0:T(8,128)S(1)} %fusion), channel_id=1, source_target_pairs={{0,50},{1,51},{2,52},{3,53},{4,54},{5,55},{6,56},{7,57},{8,58},{9,... | collective-permute-start | bytes 98312
  1164.8 33.3 %collective-permute-start.5 = (f32[16,512]{1,0:T(8,128)S(1)}, f32[16,512]{1,0:T(8,128)S(1)}, u32[]{:S(2)}, u32[]{:S(2)}) collective-permute-start(f32[16,512]{1,0:T(8,128)S(1)} %fusion), channel_id=1, source_target_pairs={{0,6},{1,7},{2,8},{3,9},{4,10},{5,11},{6,12},{7,13},{8,14},{9,15},... | collective-permute-start | bytes 98312
  1209.8 40.4 %collective-permute-start.6 = (f32[16,512]{1,0:T(8,128)S(1)}, f32[16,512]{1,0:T(8,128)S(1)}, u32[]{:S(2)}, u32[]{:S(2)}) collective-permute-start(f32[16,512]{1,0:T(8,128)S(1)} %fusion), channel_id=1, source_target_pairs={{0,7},{1,8},{2,9},{3,10},{4,11},{5,12},{6,13},{7,14},{8,15},{9,16}... | collective-permute-start | bytes 98312
  1227.1 36.2 %collective-permute-start.60 = (f32[16,512]{1,0:T(8,128)S(1)}, f32[16,512]{1,0:T(8,128)S(1)}, u32[]{:S(2)}, u32[]{:S(2)}) collective-permute-start(f32[16,512]{1,0:T(8,128)S(1)} %fusion), channel_id=1, source_target_pairs={{0,61},{1,62},{2,63},{3,64},{4,65},{5,66},{6,67},{7,68},{8,69},{9,... | collective-permute-start | bytes 98312
  1233.6 43.2 %collective-permute-start.61 = (f32[16,512]{1,0:T(8,128)S(1)}, f32[16,512]{1,0:T(8,128)S(1)}, u32[]{:S(2)}, u32[]{:S(2)}) collective-permute-start(f32[16,512]{1,0:T(8,128)S(1)} %fusion), channel_id=1, source_target_pairs={{0,62},{1,63},{2,64},{3,65},{4,66},{5,67},{6,68},{7,69},{8,70},{9,... | collective-permute-start | bytes 98312
  1235.6 41.3 %collective-permute-start.62 = (f32[16,512]{1,0:T(8,128)S(1)}, f32[16,512]{1,0:T(8,128)S(1)}, u32[]{:S(2)}, u32[]{:S(2)}) collective-permute-start(f32[16,512]{1,0:T(8,128)S(1)} %fusion), channel_id=1, source_target_pairs={{0,63},{1,64},{2,65},{3,66},{4,67},{5,68},{6,69},{7,70},{8,71},{9,... | collective-permute-start | bytes 98312
  1237.5 39.3 %collective-permute-start.7 = (f32[16,512]{1,0:T(8,128)S(1)}, f32[16,512]{1,0:T(8,128)S(1)}, u32[]{:S(2)}, u32[]{:S(2)}) collective-permute-start(f32[16,512]{1,0:T(8,128)S(1)} %fusion), channel_id=1, source_target_pairs={{0,8},{1,9},{2,10},{3,11},{4,12},{5,13},{6,14},{7,15},{8,16},{9,17... | collective-permute-start | bytes 98312
  (61 other events, 2316.7 us)
